TPU v7x, 512 devices: a whole 4x4x16 slice. The times are simulated.
512 devices in a mesh: ka: 128 (over z_lo, y, x, core), pb: 4 (over z_hi).
Axes of the slice: x: 4, y: 4, z: 16 (z_hi: 4, z_lo: 4; z = z_hi * 4 + z_lo), core: 2. Of those that a mesh axis runs over, the one named last changes fastest.
Arguments:
- coupling: float32 [256, 16, 2, 64, 128], P('ka', 'pb'), may hold values from -6 to 6
- gauge: float32 [256, 64, 128], P('ka'), may hold values from -0.5 to 0.5
- kq_index: int32 [16, 256], P(None, 'ka'), may hold values from 0 to 255, as said below
- fine_coords: int32 [3, 256], replicated, may hold values from 0 to 31
- eig_right: float32 [256, 64, 128], P('ka'), may hold values from -0.5 to 0.5
- eig_left: float32 [256, 16, 64, 128], P('ka', 'pb'), may hold values from -0.5 to 0.5
- energy_k: float32 [256, 64], P('ka'), may hold values from -4 to 4
- energy_kq: float32 [256, 16, 64], P('ka', 'pb'), may hold values from -4 to 4
- occupied: int32 [256, 16, 64], P('ka', 'pb'), may hold values 0 or 1
- frequency: float32 [16, 2], P('pb'), may hold values from 0.02 to 0.12
Outputs:
- self_energy: float32 [256, 64], P('ka')
Inputs may be any that keep to these rules, and one draw needn't show every extreme that they name: kq_index[q, k] is the number of the coarse point k displaced by the q-th window point's offset on the periodic 8 x 8 x 4 grid; for each q it is a permutation of the coarse points. Among the offsets are (4, 0, 0) and (0, 0, 3).
All inputs are finite; a program needn't handle non-finite values. No bound on the sum of `occupied` on one device may be relied on, other than what follows from the above.
Results may differ from a plain program's by a relative error of at most 0.0001.
Values sent between devices are 32-bit elements; how exact they have to be, the bound alone decides.
No kernel may reach another device: no remote copies, remote signals or barrier semaphores. Data moves between devices by JAX's collectives and lax.ppermute only.
A program may use at most 64 MiB of HBM per device.

v0:
```python
import math
import jax
import jax.numpy as jnp
from jax import lax
from jax.sharding import Mesh
from jax.sharding import PartitionSpec as P

GX = 8
GY = 8
GZ = 4
FG = 32
NK = 256
KA = ("ka_0", "ka_1", "ka_2", "ka_3")
PRECISE = lax.Precision.HIGHEST
BROADEN = 0.1
THERMAL = 0.05


def sent_to_all(x, axis):
    devices = lax.axis_size(axis)
    return lax.all_to_all(jnp.broadcast_to(x[None], (devices, *x.shape)), axis, 0, 0, tiled=True)


def joined_along(parts, dim):
    parts = jnp.moveaxis(parts, 0, dim)
    lengths = parts.shape
    return parts.reshape(*lengths[:dim], lengths[dim] * lengths[dim + 1], *lengths[dim + 2 :])


def gather_axes(x, axes, dim):
    far, near = axes
    first = sent_to_all(x, far)
    parts = jnp.swapaxes(sent_to_all(first, near), 0, 1)
    return joined_along(parts.reshape(-1, *x.shape), dim)


def taken_together(x, axis):
    return sent_to_all(x, axis).sum(axis=0)


def product(left_matrix, right_matrix):
    return jnp.dot(left_matrix, right_matrix, precision=PRECISE, preferred_element_type=jnp.float32)


def mult(pattern, first, second):
    return jnp.einsum(pattern, first, second, precision=PRECISE)


def phase_tables(fine_coords):
    points = jnp.arange(NK, dtype=jnp.int32)
    along_first = points // (GY * GZ)
    along_second = points // GZ % GY
    along_third = points % GZ
    cell_first = along_first - GX // 2
    cell_second = along_second - GY // 2
    cell_third = along_third - GZ // 2
    coarse_index = (
        cell_first[:, None] * along_first[None, :] * (GY * GZ)
        + cell_second[:, None] * along_second[None, :] * (GX * GZ)
        + cell_third[:, None] * along_third[None, :] * (GX * GY)
    ) % NK
    coarse_angles = coarse_index.astype(jnp.float32) * (2.0 * math.pi / NK)
    fine_index = (
        fine_coords[0][:, None] * cell_first[None, :]
        + fine_coords[1][:, None] * cell_second[None, :]
        + fine_coords[2][:, None] * cell_third[None, :]
    ) % FG
    fine_angles = fine_index.astype(jnp.float32) * (2.0 * math.pi / FG)
    return (
        jnp.cos(coarse_angles) / NK,
        -jnp.sin(coarse_angles) / NK,
        jnp.cos(fine_angles),
        jnp.sin(fine_angles),
    )


def right_block(matrix):
    orbitals = matrix.shape[-2]
    real_part = matrix[..., :orbitals]
    imag_part = matrix[..., orbitals:]
    upper_half = jnp.concatenate([real_part, imag_part], -1)
    lower_half = jnp.concatenate([-imag_part, real_part], -1)
    return jnp.concatenate([upper_half, lower_half], -2)


def sectioned(cols_real, cols_imag, tables):
    coarse_real, coarse_imag, fine_cos, fine_sin = tables
    space_real = product(coarse_real, cols_real) - product(coarse_imag, cols_imag)
    space_imag = product(coarse_real, cols_imag) + product(coarse_imag, cols_real)
    fine_real_part = product(fine_cos, space_real) - product(fine_sin, space_imag)
    fine_imag_part = product(fine_cos, space_imag) + product(fine_sin, space_real)
    return (fine_real_part, fine_imag_part)


def self_terms(strength, energy_k, energy_kq, occupied, frequency):
    phonon = frequency[None, :, :, None, None]
    bose_factor = 1.0 / (jnp.exp(phonon / THERMAL) - 1.0)
    filled = occupied.astype(jnp.float32)[:, :, None, :, None]
    energy_gap = energy_k[:, None, None, None, :] - energy_kq[:, :, None, :, None]
    shifted_up = energy_gap + phonon
    shifted_down = energy_gap - phonon
    kernel = (bose_factor + filled) * shifted_up / (shifted_up * shifted_up + BROADEN * BROADEN)
    kernel = kernel + (bose_factor + 1.0 - filled) * shifted_down / (
        shifted_down * shifted_down + BROADEN * BROADEN
    )
    return jnp.sum(strength / (2.0 * phonon) * kernel, axis=(1, 2, 3))


def select_rows(wanted, block_rows):
    positions = jnp.arange(block_rows.shape[0], dtype=jnp.int32)
    onehot = (wanted[:, None] == positions[None, :]).astype(jnp.float32)
    return product(onehot, block_rows.reshape(block_rows.shape[0], -1))


def shards(
    coupling,
    gauge,
    kq_index,
    fine_coords,
    eig_right,
    eig_left,
    energy_k,
    energy_kq,
    occupied,
    frequency,
):
    coarse_rows = coupling.shape[0]
    qpoint_rows = coupling.shape[1]
    branches = coupling.shape[2]
    orbitals = coupling.shape[3]
    pb_count = lax.axis_size("pb")
    tables = phase_tables(fine_coords)
    fine_total = fine_coords.shape[1]
    quarter = orbitals // pb_count
    own_part = lax.dynamic_slice_in_dim(gauge, lax.axis_index("pb") * quarter, quarter, 1)
    wanted = kq_index.T.reshape(-1)
    picked = select_rows(wanted, gather_axes(own_part, (("ka_0", "ka_1", "ka_2"), "ka_3"), 0))
    shares = picked.reshape(coarse_rows, kq_index.shape[0], quarter, 2 * orbitals)
    left_gauge = lax.all_to_all(shares, "pb", split_axis=1, concat_axis=2, tiled=True)
    right_gauge = mult("kqbjc,kcd->kqbjd", coupling, right_block(gauge))
    right_real = right_gauge[..., :orbitals]
    right_imag = right_gauge[..., orbitals:]
    left_real = left_gauge[..., :orbitals]
    left_imag = left_gauge[..., orbitals:]
    wannier_real = mult("kqjm,kqbjn->kqbmn", left_real, right_real) + mult(
        "kqjm,kqbjn->kqbmn", left_imag, right_imag
    )
    wannier_imag = mult("kqjm,kqbjn->kqbmn", left_real, right_imag) - mult(
        "kqjm,kqbjn->kqbmn", left_imag, right_real
    )
    pair_major = jnp.stack([wannier_real, wannier_imag], 1).reshape(
        coarse_rows, 2, qpoint_rows, branches, orbitals * orbitals
    )
    arrived_block = lax.all_to_all(pair_major, KA, split_axis=4, concat_axis=0, tiled=True)
    columns = arrived_block.reshape(arrived_block.shape[0], 2, -1)
    fine_real_part, fine_imag_part = sectioned(columns[:, 0], columns[:, 1], tables)
    fine_cols = jnp.stack([fine_real_part, fine_imag_part], 1).reshape(
        (fine_total, 2) + arrived_block.shape[2:]
    )
    fine_coupling = lax.all_to_all(fine_cols, KA, split_axis=0, concat_axis=4, tiled=True)
    fine_rows = fine_coupling.shape[0]
    arrived_parts = fine_coupling.reshape(fine_rows, 2, qpoint_rows, branches, orbitals, orbitals)
    coupled_real = arrived_parts[:, 0]
    coupled_imag = arrived_parts[:, 1]
    vector_real = eig_right[..., :orbitals]
    vector_imag = eig_right[..., orbitals:]
    half_real = mult("fqbjc,fcd->fqbjd", coupled_real, vector_real) - mult(
        "fqbjc,fcd->fqbjd", coupled_imag, vector_imag
    )
    half_imag = mult("fqbjc,fcd->fqbjd", coupled_real, vector_imag) + mult(
        "fqbjc,fcd->fqbjd", coupled_imag, vector_real
    )
    outer_real = eig_left[..., :orbitals]
    outer_imag = eig_left[..., orbitals:]
    bloch_real = mult("fqjm,fqbjn->fqbmn", outer_real, half_real) + mult(
        "fqjm,fqbjn->fqbmn", outer_imag, half_imag
    )
    bloch_imag = mult("fqjm,fqbjn->fqbmn", outer_real, half_imag) - mult(
        "fqjm,fqbjn->fqbmn", outer_imag, half_real
    )
    strength = bloch_real * bloch_real + bloch_imag * bloch_imag
    contrib = self_terms(strength, energy_k, energy_kq, occupied, frequency)
    summed = taken_together(contrib, "pb")
    return summed / (qpoint_rows * pb_count * orbitals)


def solution(mesh):
    split = Mesh(
        mesh.devices.reshape(4, 4, 4, 2, mesh.shape["pb"]), ("ka_0", "ka_1", "ka_2", "ka_3", "pb")
    )
    return jax.shard_map(
        shards,
        mesh=split,
        in_specs=(
            P(KA, "pb", None, None, None),
            P(KA, None, None),
            P(None, KA),
            P(),
            P(KA, None, None),
            P(KA, "pb", None, None),
            P(KA, None),
            P(KA, "pb", None),
            P(KA, "pb", None),
            P("pb", None),
        ),
        out_specs=P(KA, None),
        check_vma=False,
    )
```

profile of v0, /device:TPU:8, one launch (start us, length us, event | category | flops | bytes accessed | tf_op | source)
XLA Modules:
  0.0 292.8 jit_solution(2457836625856387109)
XLA Ops:
  0.0 0.8 constant_dynamic-slice_fusion
  0.9 38.1 %all_to_all.63 = f32[64,2,16,128]{3,2,1,0:T(8,128)S(1)} all-to-all(f32[64,2,16,128]{3,2,1,0:T(8,128)S(1)} %broadcast_in_dim.6), channel_id=1, replica_groups=mesh['ka_0'=4,'ka_1'=4,'ka_2'=4,'ka_3'=2,'pb'=4] {'ka_0','ka_1','ka_2'}, dimensions={0} | all-to-all | bytes 2097152 | tf_op jit(solution)/shard_map/all_to_all | solution.py:21
  39.2 5.4 %all_to_all.64 = f32[2,64,2,16,128]{4,3,2,1,0:T(8,128)S(1)} all-to-all(f32[2,64,2,16,128]{4,3,2,1,0:T(8,128)S(1)} %broadcast_in_dim.7), channel_id=1, replica_groups=mesh['ka_0'=4,'ka_1'=4,'ka_2'=4,'ka_3'=2,'pb'=4] {'ka_3'}, dimensions={0} | all-to-all | bytes 4194304 | tf_op jit(solution)/shard_map/all_to_all | solution.py:21
  44.9 0.9 copy.162
  45.8 1.9 copy.118
  47.7 2.8 fusion.69
  50.4 0.8 copy.119
  51.2 12.8 %all-to-all-start.2 = ((f32[2,16,16,128]{3,2,0,1:T(8,128)}), f32[2,16,16,128]{3,2,0,1:T(8,128)S(1)}, u32[]{:S(2)}, u32[]{:S(2)}) async-start(f32[2,16,16,128]{3,2,0,1:T(8,128)} %copy.119), calls=%async_computation.2 | async-start | bytes 524288 | tf_op jit(solution)/shard_map/all_to_all | solution.py:139
  64.2 0.6 convolution_bitcast_fusion
  64.8 15.0 %all-to-all-done.2 = f32[2,16,16,128]{3,2,0,1:T(8,128)S(1)} async-done(((f32[2,16,16,128]{3,2,0,1:T(8,128)}), f32[2,16,16,128]{3,2,0,1:T(8,128)S(1)}, u32[]{:S(2)}, u32[]{:S(2)}) %all-to-all-start.2) | async-done | bytes 262176 | tf_op jit(solution)/shard_map/all_to_all | solution.py:139
  79.9 1.0 fusion.20
  80.9 1.2 fusion.16
  82.1 1.2 fusion.7
  83.8 1.1 fusion.6
  85.6 16.3 %copy.127 = f32[2,2,4,2,4096]{2,3,1,0,4:T(2,128)} copy(f32[2,2,4,2,4096]{4,3,2,0,1:T(2,128)S(1)} %pad_maximum_fusion) | data formatting | bytes 1048576 | tf_op jit(solution)/shard_map/stack | solution.py:151
  101.9 27.6 %reshape.193 = f32[128,1,1024]{2,1,0:T(1,128)} reshape(f32[4096,2,2,2,4]{4,3,2,1,0:T(2,128)} %bitcast.132) | data formatting | bytes 1048576
  129.5 13.6 %all-to-all-start.3 = ((f32[128,1,1024]{2,1,0:T(1,128)}), f32[128,1,1024]{2,1,0:T(1,128)S(1)}, u32[]{:S(2)}, u32[]{:S(2)}) async-start(f32[128,1,1024]{2,1,0:T(1,128)} %reshape.193), calls=%async_computation.3 | async-start | bytes 1048576 | tf_op jit(solution)/shard_map/all_to_all | solution.py:154
  143.1 17.9 %all-to-all-done.3 = f32[128,1,1024]{2,1,0:T(1,128)S(1)} async-done(((f32[128,1,1024]{2,1,0:T(1,128)}), f32[128,1,1024]{2,1,0:T(1,128)S(1)}, u32[]{:S(2)}, u32[]{:S(2)}) %all-to-all-start.3) | async-done | bytes 524320 | tf_op jit(solution)/shard_map/all_to_all | solution.py:154
  161.5 1.9 reduce
  163.4 27.3 %reshape.194 = f32[4096,2,2,2,4]{4,3,2,1,0:T(2,128)} reshape(f32[128,1024]{1,0:T(8,128)S(1)} %reduce) | data formatting | bytes 1048576
  190.7 22.3 %copy.154 = f32[2,2,4,2,128,32]{5,4,3,2,1,0:T(8,128)S(1)} copy(f32[2,2,4,2,128,32]{2,3,1,0,5,4:T(2,128)} %bitcast.133) | data formatting | bytes 1048576 | tf_op jit(solution)/shard_map/all_to_all | solution.py:154
  213.0 3.0 %copy.129 = f32[128,2,2,4,2,32]{5,4,3,1,0,2:T(2,128)} copy(f32[128,2,2,4,2,32]{5,0,4,3,2,1:T(8,128)S(1)} %bitcast.134) | data formatting | bytes 1048576 | tf_op jit(solution)/shard_map/all_to_all | solution.py:154
  215.9 4.0 %reshape.181 = f32[256,2,256]{2,0,1:T(8,128)S(1)} reshape(f32[128,2,2,4,2,32]{5,4,3,1,0,2:T(2,128)} %copy.129) | data formatting | bytes 1048576 | tf_op jit(solution)/shard_map/reshape | solution.py:155
  219.9 1.5 fusion.34
  221.4 1.5 fusion.35
  222.9 1.5 convolution_subtract_fusion.4
  224.4 1.5 convolution_add_fusion.4
  225.9 1.6 fusion.56
  227.6 1.6 fusion.54
  229.2 1.6 convolution_subtract_fusion.3
  230.8 1.9 convolution_add_fusion.3
  232.7 1.5 copy.130
  234.3 2.8 reshape.195
  237.1 6.6 %all-to-all-start.4 = ((f32[128,1,1024]{2,1,0:T(1,128)}), f32[128,1,1024]{2,1,0:T(1,128)S(1)}, u32[]{:S(2)}, u32[]{:S(2)}) async-start(f32[128,1,1024]{2,1,0:T(1,128)} %reshape.195), calls=%async_computation.4 | async-start | bytes 1048576 | tf_op jit(solution)/shard_map/all_to_all | solution.py:160
  244.4 17.5 %all-to-all-done.4 = f32[128,1,1024]{2,1,0:T(1,128)S(1)} async-done(((f32[128,1,1024]{2,1,0:T(1,128)}), f32[128,1,1024]{2,1,0:T(1,128)S(1)}, u32[]{:S(2)}, u32[]{:S(2)}) %all-to-all-start.4) | async-done | bytes 524320 | tf_op jit(solution)/shard_map/all_to_all | solution.py:160
  261.8 1.9 reduce.1
  263.7 1.8 reshape.196
  265.5 0.7 copy.131
  266.2 1.6 copy.155
  267.8 1.8 reshape.192
  269.6 0.6 fusion.14
  271.5 0.6 convolution_subtract_fusion
  272.1 0.6 fusion.30
  272.8 0.6 fusion.32
  273.4 0.7 fusion.5
  274.1 1.0 fusion.8
  275.2 15.8 %all_to_all.65 = f32[4,1,128]{2,1,0:T(1,128)S(1)} all-to-all(f32[4,1,128]{2,1,0:T(1,128)S(1)} %reshape.197), channel_id=1, replica_groups=mesh['ka_0'=4,'ka_1'=4,'ka_2'=4,'ka_3'=2,'pb'=4] {'pb'}, dimensions={0} | all-to-all | bytes 4096 | tf_op jit(solution)/shard_map/all_to_all | solution.py:21
  291.0 0.7 reduce.2
  (53 shorter events, 5.0 us)
Async XLA Ops:
  0.0 64.2 %copy-start = (f32[2,4,2,64,128]{4,3,2,1,0:T(8,128)S(1)}, f32[2,4,2,64,128]{4,3,2,1,0:T(8,128)}, u32[]{:S(2)}) copy-start(f32[2,4,2,64,128]{4,3,2,1,0:T(8,128)} %param.10) | copy-start | bytes 1572868
  45.8 1.9 copy-start.9
  47.7 16.4 %copy-start.4 = (f32[2,64,128]{2,1,0:T(8,128)S(1)}, f32[2,64,128]{2,1,0:T(8,128)}, u32[]{:S(2)}) copy-start(f32[2,64,128]{2,1,0:T(8,128)} %param.11) | copy-start | bytes 196612
  51.2 28.6 %all-to-all-start.2 = ((f32[2,16,16,128]{3,2,0,1:T(8,128)}), f32[2,16,16,128]{3,2,0,1:T(8,128)S(1)}, u32[]{:S(2)}, u32[]{:S(2)}) async-start(f32[2,16,16,128]{3,2,0,1:T(8,128)} %copy.119), calls=%async_computation.2 | async-start | bytes 524288 | tf_op jit(solution)/shard_map/all_to_all | solution.py:139
  101.9 41.2 %copy-start.8 = (s32[3,256]{1,0:T(4,128)S(1)}, s32[3,256]{1,0:T(4,128)}, u32[]{:S(2)}) copy-start(s32[3,256]{1,0:T(4,128)} %param.13) | copy-start | bytes 9220
  129.5 31.5 %all-to-all-start.3 = ((f32[128,1,1024]{2,1,0:T(1,128)}), f32[128,1,1024]{2,1,0:T(1,128)S(1)}, u32[]{:S(2)}, u32[]{:S(2)}) async-start(f32[128,1,1024]{2,1,0:T(1,128)} %reshape.193), calls=%async_computation.3 | async-start | bytes 1048576 | tf_op jit(solution)/shard_map/all_to_all | solution.py:154
  234.2 9.5 %copy-start.7 = (f32[4,2]{0,1:T(2,128)S(1)}, f32[4,2]{0,1:T(2,128)}, u32[]{:S(2)}) copy-start(f32[4,2]{0,1:T(2,128)} %param.19) | copy-start | bytes 100
  234.2 9.8 %copy-start.6 = (s32[2,4,64]{2,1,0:T(4,128)S(1)}, s32[2,4,64]{2,1,0:T(4,128)}, u32[]{:S(2)}) copy-start(s32[2,4,64]{2,1,0:T(4,128)} %param.18) | copy-start | bytes 6148
  234.3 9.9 %copy-start.5 = (f32[2,4,64]{2,1,0:T(4,128)S(1)}, f32[2,4,64]{2,1,0:T(4,128)}, u32[]{:S(2)}) copy-start(f32[2,4,64]{2,1,0:T(4,128)} %param.17) | copy-start | bytes 6148
  234.3 9.9 %copy-start.10 = (f32[2,64]{1,0:T(2,128)S(1)}, f32[2,64]{1,0:T(2,128)}, u32[]{:S(2)}) copy-start(f32[2,64]{1,0:T(2,128)} %param.16) | copy-start | bytes 1540
  237.1 24.7 %all-to-all-start.4 = ((f32[128,1,1024]{2,1,0:T(1,128)}), f32[128,1,1024]{2,1,0:T(1,128)S(1)}, u32[]{:S(2)}, u32[]{:S(2)}) async-start(f32[128,1,1024]{2,1,0:T(1,128)} %reshape.195), calls=%async_computation.4 | async-start | bytes 1048576 | tf_op jit(solution)/shard_map/all_to_all | solution.py:160
  267.8 1.8 copy-start.3
  270.3 1.9 copy-start.2
  274.1 18.2 %copy-start.1 = (f32[2,4,2,64,128]{4,3,2,1,0:T(8,128)S(1)}, f32[2,4,2,64,128]{4,3,2,1,0:T(8,128)}, u32[]{:S(2)}) copy-start(f32[2,4,2,64,128]{4,3,2,1,0:T(8,128)} %param.10) | copy-start | bytes 1572868
where the time goes:
time: 297 us; the launch traced here: 293 us
  local copies, waits for them, and re-layouts  118 us (40%)
  blocking collectives  59.3 us (20%)
  waiting for transfers between devices  50.3 us (17%)
  starting transfers between devices  33 us (11%)
  matrix products  25.9 us (9%)
  other arithmetic  5.62 us (2%)
    unnamed x30, local copies, waits for them, and re-layouts  60.7 us
    all_to_all x3, blocking collectives, sent_to_all(): lax.all_to_all(jnp.broadcast_to(x[None], (devices, *x.shape)), axis, 0, 0...  59.3 us
    all_to_all x3, local copies, waits for them, and re-layouts, shards(): lax.all_to_all(pair_major, KA, split_axis=4, concat_axis=0, tiled=True)  25.8 us
    all_to_all x1, waiting for transfers between devices, shards(): lax.all_to_all(pair_major, KA, split_axis=4, concat_axis=0, tiled=True)  17.9 us
    all_to_all x1, waiting for transfers between devices, shards(): lax.all_to_all(fine_cols, KA, split_axis=0, concat_axis=4, tiled=True)  17.5 us
    another operation x3, local copies, waits for them, and re-layouts, shards(): jnp.stack([wannier_real, wannier_imag], 1)  16.8 us
    dot_general x9, matrix products, product(): jnp.dot(left_matrix, right_matrix, precision=PRECISE, preferred_element_t...  15.4 us
    all_to_all x1, waiting for transfers between devices, shards(): lax.all_to_all(shares, 'pb', split_axis=1, concat_axis=2, tiled=True)  15 us
  transfers between devices with their start and end apart: 3, of which 3 were waited for; matrix products, arithmetic and copies ran while one was open for 0% of the time, Pallas kernels for 0%

commit v1 on v0

--- a/solution.py
+++ b/solution.py
@@ -151,7 +151,9 @@
     pair_major = jnp.stack([wannier_real, wannier_imag], 1).reshape(
         coarse_rows, 2, qpoint_rows, branches, orbitals * orbitals
     )
-    arrived_block = lax.all_to_all(pair_major, KA, split_axis=4, concat_axis=0, tiled=True)
+    pieces = jnp.split(pair_major, lax.axis_size(KA), axis=4)
+    received = lax.all_to_all(jnp.stack(pieces), KA, 0, 0)
+    arrived_block = jnp.concatenate(received, axis=0)
     columns = arrived_block.reshape(arrived_block.shape[0], 2, -1)
     fine_real_part, fine_imag_part = sectioned(columns[:, 0], columns[:, 1], tables)
     fine_cols = jnp.stack([fine_real_part, fine_imag_part], 1).reshape(

time: 297 us -> 214 us (0.72)
  local copies, waits for them, and re-layouts: 118 us -> 34.8 us
    unnamed x30 -> x156, local copies, waits for them, and re-layouts: 60.7 us -> 20.1 us
    all_to_all x3 -> x1, local copies, waits for them, and re-layouts: 25.8 us -> 0.51 us  [shards(): received = lax.all_to_all(jnp.stack(pieces), KA, 0, 0)]
    another operation x3, local copies, waits for them, and re-layouts: 16.8 us -> 0.57 us  [shards(): jnp.stack([wannier_real, wannier_imag], 1)]
    reshape x1 -> x0, local copies, waits for them, and re-layouts: 4.01 us -> none  [shards(): columns = arrived_block.reshape(arrived_block.shape[0], 2, -1)]
  transfers between devices with their start and end apart: 3 -> 3, of which waited for: 3 -> 3; matrix products, arithmetic and copies ran while one was open for 0% -> 1% of each run, Pallas kernels for 0% -> 0%
where the time goes in v1:
time: 214 us; the launch traced here: 210 us
  blocking collectives  59.3 us (28%)
  waiting for transfers between devices  50.2 us (23%)
  local copies, waits for them, and re-layouts  34.8 us (16%)
  starting transfers between devices  32.7 us (15%)
  matrix products  25.8 us (12%)
  other arithmetic  5.36 us (3%)
    all_to_all x3, blocking collectives, sent_to_all(): lax.all_to_all(jnp.broadcast_to(x[None], (devices, *x.shape)), axis, 0, 0...  59.3 us
    unnamed x156, local copies, waits for them, and re-layouts  20.1 us
    all_to_all x1, waiting for transfers between devices, shards(): received = lax.all_to_all(jnp.stack(pieces), KA, 0, 0)  18 us
    all_to_all x1, waiting for transfers between devices, shards(): lax.all_to_all(fine_cols, KA, split_axis=0, concat_axis=4, tiled=True)  17.3 us
    dot_general x9, matrix products, product(): jnp.dot(left_matrix, right_matrix, precision=PRECISE, preferred_element_t...  15.3 us
    all_to_all x1, waiting for transfers between devices, shards(): lax.all_to_all(shares, 'pb', split_axis=1, concat_axis=2, tiled=True)  14.9 us
    all_to_all x1, starting transfers between devices, shards(): received = lax.all_to_all(jnp.stack(pieces), KA, 0, 0)  13.3 us
    all_to_all x1, starting transfers between devices, shards(): lax.all_to_all(shares, 'pb', split_axis=1, concat_axis=2, tiled=True)  12.5 us
  transfers between devices with their start and end apart: 3, of which 3 were waited for; matrix products, arithmetic and copies ran while one was open for 1% of the time, Pallas kernels for 0%

profile of v1, /device:TPU:8, one launch (start us, length us, event | category | flops | bytes accessed | tf_op | source)
XLA Modules:
  0.0 209.8 jit_solution(14012008861153002285)
XLA Ops:
  0.0 0.8 constant_dynamic-slice_fusion
  0.9 38.1 %all_to_all.53 = f32[64,2,16,128]{3,2,1,0:T(8,128)S(1)} all-to-all(f32[64,2,16,128]{3,2,1,0:T(8,128)S(1)} %broadcast_in_dim.6), channel_id=1, replica_groups=mesh['ka_0'=4,'ka_1'=4,'ka_2'=4,'ka_3'=2,'pb'=4] {'ka_0','ka_1','ka_2'}, dimensions={0} | all-to-all | bytes 2097152 | tf_op jit(solution)/shard_map/all_to_all | solution.py:21
  39.2 5.4 %all_to_all.54 = f32[2,64,2,16,128]{4,3,2,1,0:T(8,128)S(1)} all-to-all(f32[2,64,2,16,128]{4,3,2,1,0:T(8,128)S(1)} %broadcast_in_dim.7), channel_id=1, replica_groups=mesh['ka_0'=4,'ka_1'=4,'ka_2'=4,'ka_3'=2,'pb'=4] {'ka_3'}, dimensions={0} | all-to-all | bytes 4194304 | tf_op jit(solution)/shard_map/all_to_all | solution.py:21
  44.9 0.9 copy.420
  45.8 1.9 copy.369
  47.7 2.8 %fusion.69 = f32[2,16,16,128]{3,1,2,0:T(8,128)S(1)} fusion(f32[16,128,256,1]{2,1,0,3:T(8,128)} %bitcast.641, s32[2,16]{1,0:T(2,128)S(1)} %bitcast.650), kind=kOutput, calls=%fused_computation.226 | convolution fusion | flops 201334784 | bytes 2359424 | tf_op jit(solution)/shard_map/dot_general | solution.py:42
  50.4 0.8 copy.370
  51.2 12.5 %all-to-all-start.2 = ((f32[2,16,16,128]{3,2,0,1:T(8,128)}), f32[2,16,16,128]{3,2,0,1:T(8,128)S(1)}, u32[]{:S(2)}, u32[]{:S(2)}) async-start(f32[2,16,16,128]{3,2,0,1:T(8,128)} %copy.370), calls=%async_computation.2 | async-start | bytes 524288 | tf_op jit(solution)/shard_map/all_to_all | solution.py:139
  63.9 0.6 convolution_bitcast_fusion
  64.5 14.9 %all-to-all-done.2 = f32[2,16,16,128]{3,2,0,1:T(8,128)S(1)} async-done(((f32[2,16,16,128]{3,2,0,1:T(8,128)}), f32[2,16,16,128]{3,2,0,1:T(8,128)S(1)}, u32[]{:S(2)}, u32[]{:S(2)}) %all-to-all-start.2) | async-done | bytes 262176 | tf_op jit(solution)/shard_map/all_to_all | solution.py:139
  79.4 1.2 fusion.16
  80.6 1.0 fusion.20
  81.6 1.1 fusion.6
  83.2 1.2 fusion.7
  95.1 0.8 copy.378
  95.9 3.2 %reshape.189 = f32[128,1,1024]{2,1,0:T(1,128)} reshape(f32[128,2,2,4,2,32]{5,4,3,2,1,0:T(2,128)S(1)} %copy.378) | data formatting | bytes 1048576
  99.2 13.3 %all-to-all-start.3 = ((f32[128,1,1024]{2,1,0:T(1,128)}), f32[128,1,1024]{2,1,0:T(1,128)S(1)}, u32[]{:S(2)}, u32[]{:S(2)}) async-start(f32[128,1,1024]{2,1,0:T(1,128)} %reshape.189), calls=%async_computation.3 | async-start | bytes 1048576 | tf_op jit(solution)/shard_map/all_to_all | solution.py:155
  112.5 18.0 %all-to-all-done.3 = f32[128,1,1024]{2,1,0:T(1,128)S(1)} async-done(((f32[128,1,1024]{2,1,0:T(1,128)}), f32[128,1,1024]{2,1,0:T(1,128)S(1)}, u32[]{:S(2)}, u32[]{:S(2)}) %all-to-all-start.3) | async-done | bytes 524320 | tf_op jit(solution)/shard_map/all_to_all | solution.py:155
  131.0 1.9 reduce
  132.9 1.8 reshape.190
  134.6 2.0 reshape.187
  137.1 1.5 fusion.34
  138.5 1.5 fusion.35
  140.0 1.5 convolution_subtract_fusion.4
  141.5 1.5 convolution_add_fusion.4
  143.0 1.8 fusion.56
  144.8 1.6 fusion.54
  146.4 1.6 convolution_subtract_fusion.3
  148.1 1.6 convolution_add_fusion.3
  149.7 1.5 copy.380
  151.3 2.8 %reshape.191 = f32[128,1,1024]{2,1,0:T(1,128)} reshape(f32[256,2,4,2,32]{4,3,2,1,0:T(2,128)S(1)} %copy.380) | data formatting | bytes 1048576
  154.1 6.9 %all-to-all-start.4 = ((f32[128,1,1024]{2,1,0:T(1,128)}), f32[128,1,1024]{2,1,0:T(1,128)S(1)}, u32[]{:S(2)}, u32[]{:S(2)}) async-start(f32[128,1,1024]{2,1,0:T(1,128)} %reshape.191), calls=%async_computation.4 | async-start | bytes 1048576 | tf_op jit(solution)/shard_map/all_to_all | solution.py:162
  161.7 17.3 %all-to-all-done.4 = f32[128,1,1024]{2,1,0:T(1,128)S(1)} async-done(((f32[128,1,1024]{2,1,0:T(1,128)}), f32[128,1,1024]{2,1,0:T(1,128)S(1)}, u32[]{:S(2)}, u32[]{:S(2)}) %all-to-all-start.4) | async-done | bytes 524320 | tf_op jit(solution)/shard_map/all_to_all | solution.py:162
  179.0 1.9 reduce.1
  180.9 1.8 reshape.192
  182.7 0.7 copy.381
  183.4 1.6 copy.405
  185.0 1.8 reshape.188
  186.9 0.6 fusion.14
  187.5 0.6 fusion.15
  188.1 0.6 convolution_add_fusion
  188.7 0.6 convolution_subtract_fusion
  189.3 0.6 fusion.30
  190.0 0.6 fusion.32
  190.6 0.7 fusion.5
  191.3 1.0 fusion.8
  192.4 15.8 %all_to_all.55 = f32[4,1,128]{2,1,0:T(1,128)S(1)} all-to-all(f32[4,1,128]{2,1,0:T(1,128)S(1)} %reshape.193), channel_id=1, replica_groups=mesh['ka_0'=4,'ka_1'=4,'ka_2'=4,'ka_3'=2,'pb'=4] {'pb'}, dimensions={0} | all-to-all | bytes 4096 | tf_op jit(solution)/shard_map/all_to_all | solution.py:21
  208.2 0.7 reduce.2
  (179 shorter events, 13.4 us)
Async XLA Ops:
  0.0 63.9 %copy-start = (f32[2,4,2,64,128]{4,3,2,1,0:T(8,128)S(1)}, f32[2,4,2,64,128]{4,3,2,1,0:T(8,128)}, u32[]{:S(2)}) copy-start(f32[2,4,2,64,128]{4,3,2,1,0:T(8,128)} %param.10) | copy-start | bytes 1572868
  45.8 1.9 copy-start.8
  47.7 16.1 %copy-start.3 = (f32[2,64,128]{2,1,0:T(8,128)S(1)}, f32[2,64,128]{2,1,0:T(8,128)}, u32[]{:S(2)}) copy-start(f32[2,64,128]{2,1,0:T(8,128)} %param.11) | copy-start | bytes 196612
  51.2 28.2 %all-to-all-start.2 = ((f32[2,16,16,128]{3,2,0,1:T(8,128)}), f32[2,16,16,128]{3,2,0,1:T(8,128)S(1)}, u32[]{:S(2)}, u32[]{:S(2)}) async-start(f32[2,16,16,128]{3,2,0,1:T(8,128)} %copy.370), calls=%async_computation.2 | async-start | bytes 524288 | tf_op jit(solution)/shard_map/all_to_all | solution.py:139
  95.9 16.5 %copy-start.7 = (s32[3,256]{1,0:T(4,128)S(1)}, s32[3,256]{1,0:T(4,128)}, u32[]{:S(2)}) copy-start(s32[3,256]{1,0:T(4,128)} %param.13) | copy-start | bytes 9220
  99.2 31.3 %all-to-all-start.3 = ((f32[128,1,1024]{2,1,0:T(1,128)}), f32[128,1,1024]{2,1,0:T(1,128)S(1)}, u32[]{:S(2)}, u32[]{:S(2)}) async-start(f32[128,1,1024]{2,1,0:T(1,128)} %reshape.189), calls=%async_computation.3 | async-start | bytes 1048576 | tf_op jit(solution)/shard_map/all_to_all | solution.py:155
  151.2 9.8 %copy-start.6 = (f32[4,2]{0,1:T(2,128)S(1)}, f32[4,2]{0,1:T(2,128)}, u32[]{:S(2)}) copy-start(f32[4,2]{0,1:T(2,128)} %param.19) | copy-start | bytes 100
  151.3 10.1 %copy-start.5 = (s32[2,4,64]{2,1,0:T(4,128)S(1)}, s32[2,4,64]{2,1,0:T(4,128)}, u32[]{:S(2)}) copy-start(s32[2,4,64]{2,1,0:T(4,128)} %param.18) | copy-start | bytes 6148
  151.3 10.3 %copy-start.4 = (f32[2,4,64]{2,1,0:T(4,128)S(1)}, f32[2,4,64]{2,1,0:T(4,128)}, u32[]{:S(2)}) copy-start(f32[2,4,64]{2,1,0:T(4,128)} %param.17) | copy-start | bytes 6148
  151.3 10.3 %copy-start.9 = (f32[2,64]{1,0:T(2,128)S(1)}, f32[2,64]{1,0:T(2,128)}, u32[]{:S(2)}) copy-start(f32[2,64]{1,0:T(2,128)} %param.16) | copy-start | bytes 1540
  154.1 24.9 %all-to-all-start.4 = ((f32[128,1,1024]{2,1,0:T(1,128)}), f32[128,1,1024]{2,1,0:T(1,128)S(1)}, u32[]{:S(2)}, u32[]{:S(2)}) async-start(f32[128,1,1024]{2,1,0:T(1,128)} %reshape.191), calls=%async_computation.4 | async-start | bytes 1048576 | tf_op jit(solution)/shard_map/all_to_all | solution.py:162
  185.0 1.8 copy-start.2
  187.5 1.8 copy-start.1
